TPU v7x, 32 devices: a whole 2x2x4 slice. The times are simulated.
32 devices in a mesh: dp: 4 (over x, core), row: 4 (over z), col: 2 (over y).
Axes of the slice: x: 2, y: 2, z: 4, core: 2. Of those that a mesh axis runs over, the one named last changes fastest.
Arguments:
- hidden_in: float32 [1024, 32768], P('col', ('dp', 'row')), may hold values from -6 to 6
- lengths: int32 [64], P(('dp', 'row')), may hold values from 1 to 512, as said below
- ln1_gain: float32 [1024], P('col'), may hold values from 0.25 to 1.75
- ln1_shift: float32 [1024], P('col'), may hold values from -3 to 3
- w_qkv: bfloat16 [1024, 3072], P('row', 'col'), may hold values from -0.1875 to 0.1875
- bias_q: float32 [1024], P('col'), may hold values from -3 to 3
- bias_v: float32 [1024], P('col'), may hold values from -3 to 3
- w_out: bfloat16 [1024, 1024], P('col', 'row'), may hold values from -0.375 to 0.375
- bias_out: float32 [1024], P('col'), may hold values from -3 to 3
- ln2_gain: float32 [1024], P('col'), may hold values from 0.25 to 1.75
- ln2_shift: float32 [1024], P('col'), may hold values from -3 to 3
- w_up: bfloat16 [1024, 4096], P('row', 'col'), may hold values from -0.1875 to 0.1875
- bias_up: float32 [4096], P('col'), may hold values from -3 to 3
- w_down: bfloat16 [4096, 1024], P('col', 'row'), may hold values from -0.125 to 0.125
- bias_down: float32 [1024], P('col'), may hold values from -3 to 3
- cotangent: float32 [1024, 32768], P('col', ('dp', 'row')), may hold values from -6 to 6
Outputs:
- hidden_out: float32 [1024, 32768], P('col', ('dp', 'row'))
- grad_in: float32 [1024, 32768], P('col', ('dp', 'row'))
- grad_ln1_gain: float32 [1024], P('col')
- grad_ln1_shift: float32 [1024], P('col')
- grad_w_qkv: float32 [1024, 3072], P('row', 'col')
- grad_bias_q: float32 [1024], P('col')
- grad_bias_v: float32 [1024], P('col')
- grad_w_out: float32 [1024, 1024], P('col', 'row')
- grad_bias_out: float32 [1024], P('col')
- grad_ln2_gain: float32 [1024], P('col')
- grad_ln2_shift: float32 [1024], P('col')
- grad_w_up: float32 [1024, 4096], P('row', 'col')
- grad_bias_up: float32 [4096], P('col')
- grad_w_down: float32 [4096, 1024], P('col', 'row')
- grad_bias_down: float32 [1024], P('col')
Inputs may be any that keep to these rules, and one draw needn't show every extreme that they name: `lengths`: each slot holds one sequence of this many tokens followed by padding; some slot of every index pair of dp and row is full.
All inputs are finite; a program needn't handle non-finite values.
Results may differ from a plain program's by a relative error of at most 0.019.
Values may be sent and summed in bfloat16 or wider, within the bound.
A program may use at most 192 MiB of HBM per device.

v0:
```python
from functools import partial

import jax
import jax.numpy as jnp
from jax import lax
from jax.sharding import PartitionSpec as P

HEADS = 16
HEAD = 64


EPS = 1e-05
NEG = -1e30


def norm_forward(value, gain, shift):
    width = value.shape[1] * lax.axis_size("col")
    sums = lax.psum((jnp.sum(value, axis=1), jnp.sum(value * value, axis=1)), "col")
    mean = (sums[0] / width)[:, None]
    var = (sums[1] / width)[:, None] - mean * mean
    inverse = lax.rsqrt(var + EPS)
    normed = (value - mean) * inverse
    return (normed, inverse, (normed * gain + shift).astype(jnp.bfloat16))


def norm_backward(incoming, normed, inverse, gain):
    width = incoming.shape[1] * lax.axis_size("col")
    scaled = incoming * gain
    sums = lax.psum((jnp.sum(scaled, axis=1), jnp.sum(scaled * normed, axis=1)), "col")
    return inverse * (scaled - sums[0][:, None] / width - normed * sums[1][:, None] / width)


def gather_rows(value):
    return lax.all_gather(value, "col", axis=1, tiled=True)


def back_columns(value):
    return lax.psum_scatter(
        value.astype(jnp.bfloat16), "col", scatter_dimension=1, tiled=True
    ).astype(jnp.float32)


def slot_scores(slopes, query, keys, length):
    span = query.shape[0]
    pos = jnp.arange(span)
    offset = (pos[None, :] - pos[:, None]).astype(jnp.float32)
    raw = jnp.einsum("qhd,khd->hqk", query, keys, preferred_element_type=jnp.float32) * 0.125
    raw = raw + slopes[:, None, None] * offset[None]
    visible = (pos[None, :] <= pos[:, None]) & (pos[None, :] < length)
    return jnp.where(visible[None], raw, NEG)


def forward_slot(slopes, item):
    query, keys, values, length = item
    scores = slot_scores(slopes, query, keys, length)
    top = jnp.max(scores, axis=-1, keepdims=True)
    expo = jnp.exp(scores - top)
    total = jnp.sum(expo, axis=-1, keepdims=True)
    probs = expo / total
    attended = jnp.einsum(
        "hqk,khd->qhd", probs.astype(jnp.bfloat16), values, preferred_element_type=jnp.float32
    )
    return (attended, (top + jnp.log(total))[..., 0])


def backward_slot(slopes, item):
    query, keys, values, grad_out, lse, length = item
    scores = slot_scores(slopes, query, keys, length)
    probs = jnp.exp(scores - lse[..., None])
    grad_probs = jnp.einsum("qhd,khd->hqk", grad_out, values, preferred_element_type=jnp.float32)
    grad_values = jnp.einsum(
        "hqk,qhd->khd", probs.astype(jnp.bfloat16), grad_out, preferred_element_type=jnp.float32
    )
    inner = jnp.sum(probs * grad_probs, axis=-1, keepdims=True)
    grad_scores = (probs * (grad_probs - inner)).astype(jnp.bfloat16)
    grad_query = (
        jnp.einsum("hqk,khd->qhd", grad_scores, keys, preferred_element_type=jnp.float32) * 0.125
    )
    grad_keys = (
        jnp.einsum("hqk,qhd->khd", grad_scores, query, preferred_element_type=jnp.float32) * 0.125
    )
    return (grad_query, grad_keys, grad_values)


def body(
    hidden_in,
    lengths,
    ln1_gain,
    ln1_shift,
    w_qkv,
    bias_q,
    bias_v,
    w_out,
    bias_out,
    ln2_gain,
    ln2_shift,
    w_up,
    bias_up,
    w_down,
    bias_down,
    cotangent,
):
    tokens_in = jnp.transpose(hidden_in)
    grad_given = jnp.transpose(cotangent)
    rows = tokens_in.shape[0]
    slots = lengths.shape[0]
    span = rows // slots
    heads_here = w_qkv.shape[1] // (3 * HEAD)
    head_ids = lax.axis_index("col") * heads_here + jnp.arange(heads_here)
    slopes = jnp.exp2(-8.0 * (head_ids.astype(jnp.float32) + 1.0) / HEADS)
    qkv_full, up_full, out_full, down_full = (
        lax.all_gather(w_qkv, "row", axis=0, tiled=True),
        lax.all_gather(w_up, "row", axis=0, tiled=True),
        lax.all_gather(w_out, "row", axis=1, tiled=True),
        lax.all_gather(w_down, "row", axis=1, tiled=True),
    )
    normed1, inverse1, low1 = norm_forward(tokens_in, ln1_gain, ln1_shift)
    rows1 = gather_rows(low1)
    mixed = jnp.dot(rows1, qkv_full, preferred_element_type=jnp.float32).reshape(
        rows, heads_here, 3, HEAD
    )
    query = (
        (mixed[:, :, 0] + bias_q.reshape(heads_here, HEAD))
        .astype(jnp.bfloat16)
        .reshape(slots, span, heads_here, HEAD)
    )
    keys = mixed[:, :, 1].astype(jnp.bfloat16).reshape(slots, span, heads_here, HEAD)
    values = (
        (mixed[:, :, 2] + bias_v.reshape(heads_here, HEAD))
        .astype(jnp.bfloat16)
        .reshape(slots, span, heads_here, HEAD)
    )
    attended, lse = lax.map(partial(forward_slot, slopes), (query, keys, values, lengths))
    attn_low = attended.reshape(rows, heads_here * HEAD).astype(jnp.bfloat16)
    projected = lax.psum_scatter(
        jnp.dot(attn_low, out_full, preferred_element_type=jnp.float32),
        "col",
        scatter_dimension=1,
        tiled=True,
    )
    hidden1 = tokens_in + projected + bias_out
    normed2, inverse2, low2 = norm_forward(hidden1, ln2_gain, ln2_shift)
    rows2 = gather_rows(low2)
    pre = jnp.dot(rows2, up_full, preferred_element_type=jnp.float32) + bias_up
    act, act_pull = jax.vjp(partial(jax.nn.gelu, approximate=True), pre)
    act_low = act.astype(jnp.bfloat16)
    down_terms = jnp.dot(act_low, down_full, preferred_element_type=jnp.float32)
    result = (
        hidden1
        + lax.psum_scatter(
            down_terms.astype(jnp.bfloat16), "col", scatter_dimension=1, tiled=True
        ).astype(jnp.float32)
        + bias_down
    )
    grad_low = grad_given.astype(jnp.bfloat16)
    grad_full = lax.all_gather(grad_low, "col", axis=1, tiled=True)
    grad_down = jnp.einsum("tf,td->fd", act_low, grad_full, preferred_element_type=jnp.float32)
    grad_act = jnp.einsum("td,fd->tf", grad_full, down_full, preferred_element_type=jnp.float32)
    grad_pre = act_pull(grad_act)[0]
    grad_pre_low = grad_pre.astype(jnp.bfloat16)
    grad_up = jnp.einsum("td,tf->df", rows2, grad_pre_low, preferred_element_type=jnp.float32)
    grad_norm2 = back_columns(
        jnp.einsum("tf,df->td", grad_pre_low, up_full, preferred_element_type=jnp.float32)
    )
    grad_hidden1 = grad_given + norm_backward(grad_norm2, normed2, inverse2, ln2_gain)
    branch_low = grad_hidden1.astype(jnp.bfloat16)
    grad_branch = lax.all_gather(branch_low, "col", axis=1, tiled=True)
    grad_outw = jnp.einsum("tc,td->cd", attn_low, grad_branch, preferred_element_type=jnp.float32)
    grad_attn = jnp.einsum(
        "td,cd->tc", grad_branch, out_full, preferred_element_type=jnp.float32
    ).astype(jnp.bfloat16)
    grad_attn = grad_attn.reshape(slots, span, heads_here, HEAD)
    grad_query, grad_keys, grad_values = lax.map(
        partial(backward_slot, slopes), (query, keys, values, grad_attn, lse, lengths)
    )
    stacked = jnp.stack((grad_query, grad_keys, grad_values), axis=3).reshape(
        rows, 3 * heads_here * HEAD
    )
    stacked_low = stacked.astype(jnp.bfloat16)
    grad_qkv = jnp.einsum("td,tc->dc", rows1, stacked_low, preferred_element_type=jnp.float32)
    grad_norm1 = back_columns(
        jnp.einsum("tc,dc->td", stacked_low, qkv_full, preferred_element_type=jnp.float32)
    )
    grad_input = grad_hidden1 + norm_backward(grad_norm1, normed1, inverse1, ln1_gain)
    small = lax.psum(
        (
            jnp.sum(grad_norm1 * normed1, axis=0),
            jnp.sum(grad_norm1, axis=0),
            jnp.sum(grad_query.reshape(rows, heads_here * HEAD), axis=0),
            jnp.sum(grad_values.reshape(rows, heads_here * HEAD), axis=0),
            jnp.sum(grad_hidden1, axis=0),
            jnp.sum(grad_norm2 * normed2, axis=0),
            jnp.sum(grad_norm2, axis=0),
            jnp.sum(grad_pre, axis=0),
            jnp.sum(grad_given, axis=0),
        ),
        ("dp", "row"),
    )
    local = (grad_qkv, grad_up, grad_outw, grad_down)
    whole = (
        lax.psum(local[0].astype(jnp.bfloat16), "dp").astype(jnp.float32),
        lax.psum(local[1].astype(jnp.bfloat16), "dp").astype(jnp.float32),
        lax.psum(local[2].astype(jnp.bfloat16), "dp").astype(jnp.float32),
        lax.psum(local[3].astype(jnp.bfloat16), "dp").astype(jnp.float32),
    )
    summed = (
        lax.psum_scatter(
            whole[0].astype(jnp.bfloat16), "row", scatter_dimension=0, tiled=True
        ).astype(jnp.float32),
        lax.psum_scatter(
            whole[1].astype(jnp.bfloat16), "row", scatter_dimension=0, tiled=True
        ).astype(jnp.float32),
        lax.psum_scatter(
            whole[2].astype(jnp.bfloat16), "row", scatter_dimension=1, tiled=True
        ).astype(jnp.float32),
        lax.psum_scatter(
            whole[3].astype(jnp.bfloat16), "row", scatter_dimension=1, tiled=True
        ).astype(jnp.float32),
    )
    return (
        jnp.transpose(result),
        jnp.transpose(grad_input),
        small[0],
        small[1],
        summed[0],
        small[2],
        small[3],
        summed[2],
        small[4],
        small[5],
        small[6],
        summed[1],
        small[7],
        summed[3],
        small[8],
    )


def solution(mesh):
    return jax.shard_map(
        body,
        mesh=mesh,
        in_specs=(
            P("col", ("dp", "row")),
            P(("dp", "row")),
            P("col"),
            P("col"),
            P("row", "col"),
            P("col"),
            P("col"),
            P("col", "row"),
            P("col"),
            P("col"),
            P("col"),
            P("row", "col"),
            P("col"),
            P("col", "row"),
            P("col"),
            P("col", ("dp", "row")),
        ),
        out_specs=(
            P("col", ("dp", "row")),
            P("col", ("dp", "row")),
            P("col"),
            P("col"),
            P("row", "col"),
            P("col"),
            P("col"),
            P("col", "row"),
            P("col"),
            P("col"),
            P("col"),
            P("row", "col"),
            P("col"),
            P("col", "row"),
            P("col"),
        ),
        check_vma=False,
    )
```

profile of v0, /device:TPU:0, one launch (start us, length us, event | category | flops | bytes accessed | tf_op | source)
XLA Modules:
  0.0 1329.6 jit_solution(10266186835196599832)
XLA Ops:
  17.6 9.6 all-reduce.4
  34.8 53.8 %all-gather.9.cloned.1.call-done = bf16[2048,1024]{1,0:T(8,128)(2,1)} async-done(((bf16[2048,512]{1,0:T(8,128)(2,1)}), bf16[2048,1024]{1,0:T(8,128)(2,1)}) %all-gather.9.cloned.1.call-update) | async-done | bytes 4194320 | tf_op jit(solution)/shard_map/all_gather | solution.py:34
  88.6 65.1 %all-gather.11.cloned.1.call-done = bf16[1024,1536]{1,0:T(8,128)(2,1)} async-done(((bf16[256,1536]{1,0:T(8,128)(2,1)}), bf16[1024,1536]{1,0:T(8,128)(2,1)}) %all-gather.11.cloned.1.call-update) | async-done | bytes 3145744 | tf_op jit(solution)/shard_map/all_gather | solution.py:112
  153.7 9.8 fusion.100
  198.4 53.8 %while.30 = (s32[]{:T(128)}, bf16[4,512,8,64]{1,3,2,0:T(8,128)(2,1)}, f32[4,8,512]{2,1,0:T(8,128)}, bf16[4,512,8,64]{1,3,2,0:T(8,128)(2,1)}, s32[4]{0:T(128)S(1)...) while((s32[]{:T(128)}, ...), condition=%wide.region_7.8_spmd.clone.clone, body=%wide.region_4.7_spmd.clone.sunk.clone | while | flops 575664640 | bytes 49942764 | solution.py:133
  266.2 97.4 %reduce-scatter.9.cloned.1.call-done = f32[2048,512]{1,0:T(8,128)} async-done(((f32[2048,1024]{1,0:T(8,128)}), f32[2048,512]{1,0:T(8,128)}) %reduce-scatter.9.cloned.1.call-update) | async-done | bytes 4194320 | tf_op jit(solution)/shard_map/reduce_scatter | solution.py:135
  390.5 55.4 %all-gather.17.cloned.1.call-done = bf16[1024,2048]{1,0:T(8,128)(2,1)} async-done(((bf16[256,2048]{1,0:T(8,128)(2,1)}), bf16[1024,2048]{1,0:T(8,128)(2,1)}) %all-gather.17.cloned.1.call-update) | async-done | bytes 4194320 | tf_op jit(solution)/shard_map/all_gather | solution.py:113
  445.9 56.8 %all-gather.15.cloned.1.call-done = bf16[2048,1024]{1,0:T(8,128)(2,1)} async-done(((bf16[2048,512]{1,0:T(8,128)(2,1)}), bf16[2048,1024]{1,0:T(8,128)(2,1)}) %all-gather.15.cloned.1.call-update) | async-done | bytes 4194320 | tf_op jit(solution)/shard_map/all_gather | solution.py:34
  502.7 15.3 %fusion.102 = f32[2048,2048]{1,0:T(8,128)} fusion(bf16[2048,1024]{1,0:T(8,128)(2,1)} %all-gather.15.cloned.1.call-done, bf16[1024,2048]{1,0:T(8,128)(2,1)} %all-gather.17.cloned.1.call-done), kind=kOutput, calls=%fused_computation.144 | convolution fusion | flops 8589934592 | bytes 25165824 | tf_op jit(solution)/shard_map/dot_general | solution.py:144
  517.9 43.1 %all-gather.21.cloned.1.call-done = bf16[2048,1024]{1,0:T(8,128)(2,1)} async-done(((bf16[2048,512]{1,0:T(8,128)(2,1)}), bf16[2048,1024]{1,0:T(8,128)(2,1)}) %all-gather.21.cloned.1.call-update) | async-done | bytes 4194320 | tf_op jit(solution)/shard_map/all_gather | solution.py:156
  561.1 82.2 %all-gather.19.cloned.1.call-done = bf16[2048,1024]{1,0:T(8,128)(2,1)} async-done(((bf16[2048,256]{1,0:T(8,128)(2,1)}), bf16[2048,1024]{1,0:T(8,128)(2,1)}) %all-gather.19.cloned.1.call-update) | async-done | bytes 4194320 | tf_op jit(solution)/shard_map/all_gather | solution.py:115
  643.3 27.5 %fusion.91 = (f32[2048]{0:T(1024)}, bf16[2048,2048]{1,0:T(8,128)(2,1)}, bf16[2048,2048]{1,0:T(8,128)(2,1)}) fusion(f32[2048,2048]{1,0:T(8,128)} %fusion.102, f32[2048]{0:T(1024)S(1)} %copy-done.34, bf16[2048,1024]{1,0:T(8,128)(2,1)} %all-gather.21.cloned.1.call-done, bf16[2048,1024]{1,0:T(8,128)(2,1)} %all-gather.19.cloned.1.call-done), kind=kOutput, calls=%fused_computation.136 | convolution fusion | flops 8690595840 | bytes 41959424 | tf_op jit(solution)/shard_map/td,fd->tf/dot_general | solution.py:158
  670.8 12.8 fusion.84
  683.7 13.8 %convolution_convert_fusion.2 = bf16[2048,1024]{1,0:T(8,128)(2,1)} fusion(bf16[2048,2048]{1,0:T(8,128)(2,1)} %get-tuple-element.304, bf16[2048,1024]{1,0:T(8,128)(2,1)} %all-gather.19.cloned.1.call-done), kind=kOutput, calls=%fused_computation.122 | convolution fusion | flops 8592031744 | bytes 16777216 | tf_op jit(solution)/shard_map/dot_general | solution.py:147
  697.6 38.7 %reduce-scatter.13.cloned.1.call-done = bf16[2048,512]{1,0:T(8,128)(2,1)} async-done(((bf16[2048,1024]{1,0:T(8,128)(2,1)}), bf16[2048,512]{1,0:T(8,128)(2,1)}) %reduce-scatter.13.cloned.1.call-update) | async-done | bytes 2097168 | tf_op jit(solution)/shard_map/reduce_scatter | solution.py:38
  748.0 44.8 %reduce-scatter.11.cloned.1.call-done = bf16[2048,512]{1,0:T(8,128)(2,1)} async-done(((bf16[2048,1024]{1,0:T(8,128)(2,1)}), bf16[2048,512]{1,0:T(8,128)(2,1)}) %reduce-scatter.11.cloned.1.call-update) | async-done | bytes 2097168 | tf_op jit(solution)/shard_map/reduce_scatter | solution.py:150
  792.9 8.2 fusion.93
  804.7 14.4 %convolution_convert_fusion.3 = bf16[2048,1024]{1,0:T(8,128)(2,1)} fusion(bf16[2048,2048]{1,0:T(8,128)(2,1)} %get-tuple-element.304, bf16[2048,1024]{1,0:T(8,128)(2,1)} %all-gather.21.cloned.1.call-done), kind=kOutput, calls=%fused_computation.123 | convolution fusion | flops 8592031744 | bytes 16777216 | tf_op jit(solution)/shard_map/tf,td->fd/dot_general | solution.py:157
  819.2 14.1 %fusion.87 = bf16[1024,2048]{1,0:T(8,128)(2,1)} fusion(bf16[2048,1024]{1,0:T(8,128)(2,1)} %all-gather.15.cloned.1.call-done, bf16[2048,2048]{1,0:T(8,128)(2,1)} %get-tuple-element.296), kind=kOutput, calls=%fused_computation.121 | convolution fusion | flops 8592031744 | bytes 16777216 | tf_op jit(solution)/shard_map/td,tf->df/dot_general | solution.py:161
  833.3 28.3 %all-gather.23.cloned.1.call-done = bf16[2048,1024]{1,0:T(8,128)(2,1)} async-done(((bf16[2048,512]{1,0:T(8,128)(2,1)}), bf16[2048,1024]{1,0:T(8,128)(2,1)}) %all-gather.23.cloned.1.call-update) | async-done | bytes 4194320 | tf_op jit(solution)/shard_map/all_gather | solution.py:167
  880.8 133.3 %while.31 = (s32[]{:T(128)}, f32[4,512,8,64]{1,3,2,0:T(8,128)}, bf16[4,512,8,64]{1,3,2,0:T(8,128)(2,1)}, f32[4,512,8,64]{1,3,2,0:T(8,128)}, bf16[4,512,8,64]{1,3...) while((s32[]{:T(128)}, f32[4,512,8,64]{1,3,2,0:T(8,128)}, ...), condition=%wide.region_21.22_spmd.clone.clone, body=%wide.region_19.21_spmd.clone.sunk.clone | while | flops 1366815232 | bytes 122771752 | solution.py:173
  885.4 8.9 multiply_reduce_fusion.4
  918.8 8.9 multiply_reduce_fusion.4
  952.1 8.9 multiply_reduce_fusion.4
  985.4 8.9 multiply_reduce_fusion.4
  1022.2 8.3 copy.58
  1038.9 8.5 convolution_convert_fusion
  1050.8 61.7 %reduce-scatter.17.cloned.1.call-done = bf16[256,1536]{1,0:T(8,128)(2,1)} async-done(((bf16[1024,1536]{1,0:T(8,128)(2,1)}), bf16[256,1536]{1,0:T(8,128)(2,1)}) %reduce-scatter.17.cloned.1.call-update) | async-done | bytes 786448 | tf_op jit(solution)/shard_map/reduce_scatter | solution.py:207
  1112.5 11.7 convolution_convert_fusion.1
  1132.3 51.7 %all-reduce.8.cloned.1.call-done = (bf16[256,1536]{1,0:T(8,128)(2,1)}, bf16[512,256]{1,0:T(8,128)(2,1)}, bf16[256,2048]{1,0:T(8,128)(2,1)}, bf16[2048,256]{1,0:T(8,128)(2,1)}) async-done(((bf16[256,1536]{1,0:T(8,128)(2,1)}, bf16[512,256]{1,0:T(8,128)(2,1)}, bf16[256,2048]{1,0:T(8,128)(2,1)}, bf16[2048,256]{1,0:T(8,128)(2,1)}), (bf16[256,1536]{1,0:T(8,128)(2,1)}, bf16[512,256]{1,0:T(8,128)(2,1)}, ...) | async-done | bytes 3145744 | tf_op jit(solution)/shard_map/psum | solution.py:201
  1192.6 47.9 %reduce-scatter.15.cloned.1.call-done = bf16[2048,512]{1,0:T(8,128)(2,1)} async-done(((bf16[2048,1024]{1,0:T(8,128)(2,1)}), bf16[2048,512]{1,0:T(8,128)(2,1)}) %reduce-scatter.15.cloned.1.call-update) | async-done | bytes 2097168 | tf_op jit(solution)/shard_map/reduce_scatter | solution.py:38
  1262.7 59.9 %all-reduce = (f32[512]{0:T(512)}, f32[512]{0:T(512)}, f32[512]{0:T(512)}, f32[512]{0:T(512)}, f32[512]{0:T(512)}, /*index=5*/f32[512]{0:T(512)}, f32[512]{0:T(512)}, f32[2048]{0:T(1024)}, f32[512]{0:T(512)}) all-reduce(f32[512]{0:T(512)S(1)} %get-tuple-element.228, ...), channel_id=1, replica_groups=mesh['dp'=4,'row'=4,'col'=2] {'dp','row'}, use_global_device_ids=true, to_apply=%region_28.29 | all-reduce | flops 6144 | bytes 49152 | tf_op jit(solution)/shard_map/psum | solution.py:185
  (278 shorter events, 337.4 us)
Async XLA Ops:
  7.2 81.4 %all-gather.9.cloned.1.call-start = ((), (), s32[]{:S(2)}) async-start(), calls=%async_computation.8 | async-start | bytes 6291456 | tf_op jit(solution)/shard_map/all_gather | solution.py:34
  12.6 15.2 %copy-start.19 = (f32[512]{0:T(512)S(1)}, f32[512]{0:T(512)}, u32[]{:S(2)}) copy-start(f32[512]{0:T(512)} %param.22) | copy-start | bytes 6148
  12.6 15.2 %copy-start.25 = (f32[512]{0:T(512)S(1)}, f32[512]{0:T(512)}, u32[]{:S(2)}) copy-start(f32[512]{0:T(512)} %param.23) | copy-start | bytes 6148
  31.4 122.2 %all-gather.11.cloned.1.call-start = ((), (), s32[]{:S(2)}) async-start(), calls=%async_computation.9 | async-start | bytes 3932160 | tf_op jit(solution)/shard_map/all_gather | solution.py:112
  32.2 225.9 %all-gather.13.cloned.1.call-start = ((), (), s32[]{:S(2)}) async-start(), calls=%async_computation.10 | async-start | bytes 1310720 | tf_op jit(solution)/shard_map/all_gather | solution.py:114
  32.9 330.7 %reduce-scatter.9.cloned.1.call-start = ((), (), s32[]{:S(2)}) async-start(), calls=%async_computation.11 | async-start | bytes 12582912 | tf_op jit(solution)/shard_map/reduce_scatter | solution.py:135
  33.2 130.3 %copy-start.3 = (bf16[4,512,8,64]{1,3,2,0:T(8,128)(2,1)}, bf16[4,512,8,64]{1,3,2,0:T(8,128)(2,1)S(1)}, u32[]{:S(2)}) copy-start(bf16[4,512,8,64]{1,3,2,0:T(8,128)(2,1)S(1)} %fusion.99) | copy-start | bytes 6291460
  265.6 98.1 %copy-start.30 = (f32[512]{0:T(512)S(1)}, f32[512]{0:T(512)}, u32[]{:S(2)}) copy-start(f32[512]{0:T(512)} %param.28) | copy-start | bytes 6148
  265.6 180.3 %all-gather.17.cloned.1.call-start = ((), (), s32[]{:S(2)}) async-start(), calls=%async_computation.13 | async-start | bytes 5242880 | tf_op jit(solution)/shard_map/all_gather | solution.py:113
  266.2 110.3 %copy-start.18 = (f32[512]{0:T(512)S(1)}, f32[512]{0:T(512)}, u32[]{:S(2)}) copy-start(f32[512]{0:T(512)} %param.29) | copy-start | bytes 6148
  266.2 110.3 %copy-start.26 = (f32[512]{0:T(512)S(1)}, f32[512]{0:T(512)}, u32[]{:S(2)}) copy-start(f32[512]{0:T(512)} %param.30) | copy-start | bytes 6148
  266.2 236.5 %all-gather.15.cloned.1.call-start = ((), (), s32[]{:S(2)}) async-start(), calls=%async_computation.12 | async-start | bytes 6291456 | tf_op jit(solution)/shard_map/all_gather | solution.py:34
  380.2 180.9 %all-gather.21.cloned.1.call-start = ((), (), s32[]{:S(2)}) async-start(), calls=%async_computation.16 | async-start | bytes 6291456 | tf_op jit(solution)/shard_map/all_gather | solution.py:156
  389.7 253.7 %all-gather.19.cloned.1.call-start = ((), (), s32[]{:S(2)}) async-start(), calls=%async_computation.14 | async-start | bytes 5242880 | tf_op jit(solution)/shard_map/all_gather | solution.py:115
  390.4 252.9 %copy-start.34 = (f32[2048]{0:T(1024)S(1)}, f32[2048]{0:T(1024)}, u32[]{:S(2)}) copy-start(f32[2048]{0:T(1024)} %param.32) | copy-start | bytes 24580
  390.4 345.9 %reduce-scatter.13.cloned.1.call-start = ((), (), s32[]{:S(2)}) async-start(), calls=%async_computation.17 | async-start | bytes 6291456 | tf_op jit(solution)/shard_map/reduce_scatter | solution.py:38
  643.3 27.5 %copy-start.32 = (bf16[1024,2048]{1,0:T(8,128)(2,1)S(1)}, bf16[1024,2048]{1,0:T(8,128)(2,1)}, u32[]{:S(2)}) copy-start(bf16[1024,2048]{1,0:T(8,128)(2,1)} %all-gather.17.cloned.1.call-done) | copy-start | bytes 12582916
  683.6 109.2 %reduce-scatter.11.cloned.1.call-start = ((), (), s32[]{:S(2)}) async-start(), calls=%async_computation.15 | async-start | bytes 6291456 | tf_op jit(solution)/shard_map/reduce_scatter | solution.py:150
  697.5 95.4 %copy-start.27 = (f32[512]{0:T(512)S(1)}, f32[512]{0:T(512)}, u32[]{:S(2)}) copy-start(f32[512]{0:T(512)} %param.34) | copy-start | bytes 6148
  697.5 164.1 %all-gather.23.cloned.1.call-start = ((), (), s32[]{:S(2)}) async-start(), calls=%async_computation.18 | async-start | bytes 6291456 | tf_op jit(solution)/shard_map/all_gather | solution.py:167
  736.3 56.6 %copy-start.7 = (bf16[2048,512]{1,0:T(8,128)(2,1)S(1)}, bf16[2048,512]{1,0:T(8,128)(2,1)}, u32[]{:S(2)}) copy-start(bf16[2048,512]{1,0:T(8,128)(2,1)} %reduce-scatter.13.cloned.1.call-done) | copy-start | bytes 6291460
  804.6 242.8 %reduce-scatter.23.cloned.1.call-start = ((), (), s32[]{:S(2)}) async-start(), calls=%async_computation.23 | async-start | bytes 5242880 | tf_op jit(solution)/shard_map/reduce_scatter | solution.py:216
  819.1 228.4 %reduce-scatter.21.cloned.1.call-start = ((), (), s32[]{:S(2)}) async-start(), calls=%async_computation.22 | async-start | bytes 5242880 | tf_op jit(solution)/shard_map/reduce_scatter | solution.py:210
  833.3 28.4 %copy-start.33 = (bf16[512,1024]{1,0:T(8,128)(2,1)S(1)}, bf16[512,1024]{1,0:T(8,128)(2,1)}, u32[]{:S(2)}) copy-start(bf16[512,1024]{1,0:T(8,128)(2,1)} %all-gather.13.cloned.1.call-done) | copy-start | bytes 3145732
  833.3 217.5 %reduce-scatter.19.cloned.1.call-start = ((), (), s32[]{:S(2)}) async-start(), calls=%async_computation.21 | async-start | bytes 1310720 | tf_op jit(solution)/shard_map/reduce_scatter | solution.py:213
  1014.2 98.3 %reduce-scatter.17.cloned.1.call-start = ((), (), s32[]{:S(2)}) async-start(), calls=%async_computation.20 | async-start | bytes 3932160 | tf_op jit(solution)/shard_map/reduce_scatter | solution.py:207
  1047.4 136.6 %all-reduce.8.cloned.1.call-start = ((), (), s32[]{:S(2)}) async-start(), calls=%async_computation.24 | async-start | bytes 6291456 | tf_op jit(solution)/shard_map/psum | solution.py:201
  1112.5 128.0 %reduce-scatter.15.cloned.1.call-start = ((), (), s32[]{:S(2)}) async-start(), calls=%async_computation.19 | async-start | bytes 6291456 | tf_op jit(solution)/shard_map/reduce_scatter | solution.py:38
  1185.8 54.7 %copy-start.15 = (f32[2048]{0:T(1024)S(1)}, f32[2048]{0:T(1024)}, u32[]{:S(2)}) copy-start(f32[2048]{0:T(1024)} %copy-done.14) | copy-start | bytes 24580
  1185.8 54.7 %copy-start.17 = (f32[2048]{0:T(1024)S(1)}, f32[2048]{0:T(1024)}, u32[]{:S(2)}) copy-start(f32[2048]{0:T(1024)} %copy-done.16) | copy-start | bytes 24580
  1185.8 54.7 %copy-start.20 = (f32[512]{0:T(512)S(1)}, f32[512]{0:T(512)}, u32[]{:S(2)}) copy-start(f32[512]{0:T(512)} %param.22) | copy-start | bytes 6148
  1240.5 11.2 copy-start.8
  (37 other events, 166.0 us)
Sparse Core Ops, SparseCore 0:
  31.5 56.9 all-gather.8
  90.1 63.4 all-gather.10
  155.2 28.8 all-gather.12
  265.7 97.8 reduce-scatter.8
  365.1 80.7 all-gather.16
  447.4 55.2 all-gather.14
  504.3 56.7 all-gather.20
  562.7 80.5 all-gather.18
  683.8 52.4 reduce-scatter.12
  738.4 54.3 reduce-scatter.10
  804.8 56.8 all-gather.22
  863.9 76.7 reduce-scatter.22
  943.0 77.2 reduce-scatter.20
  1023.1 27.6 reduce-scatter.18
  1053.5 58.8 reduce-scatter.16
  1114.9 68.9 all-reduce.7
  1186.1 54.3 reduce-scatter.14
where the time goes:
time: 1340 us; the launch traced here: 1330 us
  waiting for transfers between devices  733 us (55%)
  matrix products  270 us (20%)
  other arithmetic  124 us (9%)
  local copies, waits for them, and re-layouts  96.5 us (7%)
  blocking collectives  90.2 us (7%)
  between operations  14.7 us (1%)
    all_gather x2, waiting for transfers between devices, gather_rows(): return lax.all_gather(value, 'col', axis=1, tiled=True)  111 us
    reduce_scatter x1, waiting for transfers between devices, body(): lax.psum_scatter(jnp.dot(attn_low, out_full, preferred_element_type=jnp.f...  97.4 us
    reduce_scatter x2, waiting for transfers between devices, back_columns(): lax.psum_scatter(value.astype(jnp.bfloat16), 'col', scatter_dimension=1,...  86.7 us
    all_gather x1, waiting for transfers between devices, body(): lax.all_gather(w_down, 'row', axis=1, tiled=True)  82.2 us
    all_gather x1, waiting for transfers between devices, body(): lax.all_gather(w_qkv, 'row', axis=0, tiled=True)  65.1 us
    reduce_scatter x1, waiting for transfers between devices, body(): lax.psum_scatter(whole[0].astype(jnp.bfloat16), 'row', scatter_dimension=...  61.7 us
    psum x1, blocking collectives, body(): lax.psum((jnp.sum(grad_norm1 * normed1, axis=0), jnp.sum(grad_norm1, axis...  59.9 us
    all_gather x1, waiting for transfers between devices, body(): lax.all_gather(w_up, 'row', axis=0, tiled=True)  55.4 us
  transfers between devices with their start and end apart: 17, of which 14 were waited for; matrix products, arithmetic and copies ran while one was open for 30% of the time, Pallas kernels for 0%

commit v1 on v0

--- a/solution.py
+++ b/solution.py
@@ -3,6 +3,8 @@
 import jax
 import jax.numpy as jnp
 from jax import lax
+from jax.experimental import pallas as pl
+from jax.experimental.pallas import tpu as pltpu
 from jax.sharding import PartitionSpec as P
 
 HEADS = 16
@@ -82,7 +84,7 @@
     return (grad_query, grad_keys, grad_values)
 
 
-def body(
+def wide_body(
     hidden_in,
     lengths,
     ln1_gain,
@@ -236,9 +238,391 @@
     )
 
 
+def slot_terms(slope, query, keys, length, first, block):
+    span = first + block
+    raw = lax.dot_general(
+        keys[:, :span], query, (((0,), (0,)), ((), ())), preferred_element_type=jnp.float32
+    )
+    key_pos = lax.broadcasted_iota(jnp.int32, (span, 1), 0)
+    bias = jnp.where(key_pos < length, slope * key_pos.astype(jnp.float32), NEG)
+    key_all = lax.broadcasted_iota(jnp.int32, (span, block), 0)
+    query_all = lax.broadcasted_iota(jnp.int32, (span, block), 1) + first
+    return jnp.where(key_all <= query_all, raw + bias, NEG)
+
+
+def attend_kernel(lengths, slopes, mixed_ref, attn_ref, lse_ref):
+    length = lengths[pl.program_id(1)]
+    span = mixed_ref.shape[2]
+    block = span // 2
+    for head in range(mixed_ref.shape[0]):
+        slope = slopes[pl.program_id(0) * mixed_ref.shape[0] + head]
+        for first in (0, block):
+            end = first + block
+            query = mixed_ref[head, :HEAD, first:end] * 0.125
+            scores = slot_terms(slope, query, mixed_ref[head, HEAD : 2 * HEAD], length, first, block)
+            top = jnp.max(scores, axis=0, keepdims=True)
+            expo = jnp.exp(scores - top)
+            total = jnp.sum(expo, axis=0, keepdims=True)
+            attended = jnp.dot(
+                mixed_ref[head, 2 * HEAD :, :end],
+                expo.astype(jnp.bfloat16),
+                preferred_element_type=jnp.float32,
+            )
+            attn_ref[head, :, first:end] = (attended / total).astype(jnp.bfloat16)
+            lse_ref[head, :, first:end] = top + jnp.log(total)
+
+
+def attend_back_kernel(lengths, slopes, mixed_ref, grad_ref, lse_ref, out_ref):
+    length = lengths[pl.program_id(1)]
+    span = mixed_ref.shape[2]
+    block = span // 2
+    over_queries = (((1,), (1,)), ((), ()))
+    for head in range(mixed_ref.shape[0]):
+        slope = slopes[pl.program_id(0) * mixed_ref.shape[0] + head]
+        terms = []
+        for first in (0, block):
+            end = first + block
+            query = mixed_ref[head, :HEAD, first:end] * 0.125
+            grad = grad_ref[head, :, first:end]
+            keys = mixed_ref[head, HEAD : 2 * HEAD]
+            scores = slot_terms(slope, query, keys, length, first, block)
+            probs = jnp.exp(scores - lse_ref[head, :, first:end])
+            grad_probs = lax.dot_general(
+                mixed_ref[head, 2 * HEAD :, :end],
+                grad,
+                (((0,), (0,)), ((), ())),
+                preferred_element_type=jnp.float32,
+            )
+            inner = jnp.sum(probs * grad_probs, axis=0, keepdims=True)
+            grad_scores = (probs * (grad_probs - inner)).astype(jnp.bfloat16)
+            grad_query = jnp.dot(keys[:, :end], grad_scores, preferred_element_type=jnp.float32)
+            out_ref[head, :HEAD, first:end] = (grad_query * 0.125).astype(jnp.bfloat16)
+            terms.append(
+                (
+                    lax.dot_general(
+                        query, grad_scores, over_queries, preferred_element_type=jnp.float32
+                    ),
+                    lax.dot_general(
+                        grad,
+                        probs.astype(jnp.bfloat16),
+                        over_queries,
+                        preferred_element_type=jnp.float32,
+                    ),
+                )
+            )
+        for which in (0, 1):
+            low = HEAD * (1 + which)
+            early, late = terms[0][which], terms[1][which]
+            out_ref[head, low : low + HEAD, :block] = (early + late[:, :block]).astype(jnp.bfloat16)
+            out_ref[head, low : low + HEAD, block:] = late[:, block:].astype(jnp.bfloat16)
+
+
+HEADS_STEP = 2
+
+
+def per_head(rows, span):
+    return pl.BlockSpec((HEADS_STEP, rows, span), lambda h, s, *_: (h, 0, s))
+
+
+def attend(lengths, slopes, mixed):
+    heads, depth, rows = mixed.shape
+    slots = lengths.shape[0]
+    span = rows // slots
+    return pl.pallas_call(
+        attend_kernel,
+        grid_spec=pltpu.PrefetchScalarGridSpec(
+            num_scalar_prefetch=2,
+            grid=(heads // HEADS_STEP, slots),
+            in_specs=[per_head(depth, span)],
+            out_specs=[per_head(HEAD, span), per_head(1, span)],
+        ),
+        out_shape=[
+            jax.ShapeDtypeStruct((heads, HEAD, rows), jnp.bfloat16),
+            jax.ShapeDtypeStruct((heads, 1, rows), jnp.float32),
+        ],
+        cost_estimate=pl.CostEstimate(
+            flops=16 * heads * rows * span * HEAD, bytes_accessed=16 * 2**20, transcendentals=0
+        ),
+    )(lengths, slopes, mixed)
+
+
+def attend_back(lengths, slopes, mixed, grad, lse):
+    heads, depth, rows = mixed.shape
+    slots = lengths.shape[0]
+    span = rows // slots
+    return pl.pallas_call(
+        attend_back_kernel,
+        grid_spec=pltpu.PrefetchScalarGridSpec(
+            num_scalar_prefetch=2,
+            grid=(heads // HEADS_STEP, slots),
+            in_specs=[per_head(depth, span), per_head(HEAD, span), per_head(1, span)],
+            out_specs=per_head(depth, span),
+        ),
+        out_shape=jax.ShapeDtypeStruct(mixed.shape, jnp.bfloat16),
+        cost_estimate=pl.CostEstimate(
+            flops=40 * heads * rows * span * HEAD, bytes_accessed=32 * 2**20, transcendentals=0
+        ),
+    )(lengths, slopes, mixed, grad, lse)
+
+
+def swap(value, axis):
+    if axis == "y":
+        return lax.ppermute(value, "col", [(i, i ^ 1) for i in range(lax.axis_size("col"))])
+    step = {"core": 1, "x": 2}[axis]
+    return lax.ppermute(value, "dp", [(i, i ^ step) for i in range(lax.axis_size("dp"))])
+
+
+def spread(piece, order):
+    held = piece[None]
+    for axis in (*order, "core"):
+        held = jnp.concatenate((held, swap(held, axis)), axis=0)
+    return held
+
+
+def collect(near, far, order):
+    held = (near.astype(jnp.float32) + swap(far, "core").astype(jnp.float32)).astype(jnp.bfloat16)
+    for axis in (order[1], order[0]):
+        half = held.shape[0] // 2
+        other = swap(held[half:], axis)
+        held = (held[:half].astype(jnp.float32) + other.astype(jnp.float32)).astype(jnp.bfloat16)
+    return held[0]
+
+
+def places(order):
+    index = jnp.arange(8)
+    bit = {"core": index // 4, order[1]: index // 2 % 2, order[0]: index % 2}
+    dp = lax.axis_index("dp") ^ (2 * bit["x"] + bit["core"])
+    return 4 * (lax.axis_index("col") ^ bit["y"]) + dp
+
+
+def stats(value):
+    width = value.shape[0]
+    mean = jnp.sum(value, axis=0, keepdims=True) / width
+    var = jnp.sum(value * value, axis=0, keepdims=True) / width - mean * mean
+    return mean, lax.rsqrt(var + EPS)
+
+
+def norm_back(incoming, normed, inverse, gain):
+    width = incoming.shape[0]
+    scaled = incoming * gain
+    first = jnp.sum(scaled, axis=0, keepdims=True) / width
+    second = jnp.sum(scaled * normed, axis=0, keepdims=True) / width
+    return inverse * (scaled - first - normed * second)
+
+
+HEAD_ORDER = ("y", "x")
+UP_ORDER = ("x", "y")
+
+
+def body(
+    hidden_in,
+    lengths,
+    ln1_gain,
+    ln1_shift,
+    w_qkv,
+    bias_q,
+    bias_v,
+    w_out,
+    bias_out,
+    ln2_gain,
+    ln2_shift,
+    w_up,
+    bias_up,
+    w_down,
+    bias_down,
+    cotangent,
+):
+    low, f32 = jnp.bfloat16, jnp.float32
+    col, dp = lax.axis_index("col"), lax.axis_index("dp")
+    part, rows = hidden_in.shape[0], hidden_in.shape[1] // 2
+    slots = lengths.shape[0] // 2
+    lengths = lax.dynamic_slice(lengths, (col * slots,), (slots,))
+
+    def quarter(value, axis):
+        size = value.shape[axis] // 4
+        return lax.dynamic_slice_in_dim(value, dp * size, size, axis)
+
+    piece_qkv = lax.all_gather(quarter(w_qkv, 1), "row", axis=0, tiled=True)
+    piece_out = lax.all_gather(quarter(w_out, 0), "row", axis=1, tiled=True)
+    piece_up = lax.all_gather(quarter(w_up, 1), "row", axis=0, tiled=True)
+    piece_down = lax.all_gather(quarter(w_down, 0), "row", axis=1, tiled=True)
+
+    def both(mine, other, axis):
+        return jnp.where(
+            col == 0,
+            jnp.concatenate((mine, other), axis=axis),
+            jnp.concatenate((other, mine), axis=axis),
+        )
+
+    def to_tokens(value):
+        mine = lax.dynamic_slice_in_dim(value, col * rows, rows, 1)
+        send = lax.dynamic_slice_in_dim(value, (1 - col) * rows, rows, 1).astype(low)
+        return both(mine, swap(send, "y").astype(f32), 0)
+
+    def to_features(value):
+        mine = lax.dynamic_slice_in_dim(value, col * part, part, 0)
+        send = lax.dynamic_slice_in_dim(value, (1 - col) * part, part, 0).astype(low)
+        return both(mine, swap(send, "y").astype(f32), 1)
+
+    small_in = (
+        ln1_gain, ln1_shift, bias_q, bias_v, bias_out, ln2_gain, ln2_shift, bias_down, bias_up
+    )
+    packed = jnp.concatenate(small_in)
+    pair = both(packed[None], swap(packed, "y")[None], 0)
+    cuts = [0]
+    for value in small_in:
+        cuts.append(cuts[-1] + value.shape[0])
+    full = [pair[:, a:b].reshape(-1) for a, b in zip(cuts, cuts[1:])]
+    gain1, shift1, full_q, full_v, full_out, gain2, shift2, full_down, full_up = full
+    head_at, up_at = places(HEAD_ORDER), places(UP_ORDER)
+    pair_heads = HEADS // 8
+    bias_qv = jnp.stack(
+        (full_q.reshape(HEADS, HEAD), jnp.zeros((HEADS, HEAD), f32), full_v.reshape(HEADS, HEAD)),
+        axis=1,
+    ).reshape(8, pair_heads * 3 * HEAD)[head_at]
+    head_ids = (head_at[:, None] * pair_heads + jnp.arange(pair_heads)).reshape(HEADS)
+    slopes = jnp.exp2(-8.0 * (head_ids.astype(f32) + 1.0) / HEADS)
+    bias_hidden = full_up.reshape(8, -1)[up_at]
+
+    tokens = to_tokens(hidden_in)
+    wide_qkv = spread(piece_qkv, HEAD_ORDER)
+    wide_out = spread(piece_out, HEAD_ORDER)
+    wide_up = spread(piece_up, UP_ORDER)
+    wide_down = spread(piece_down, UP_ORDER)
+    grad_given = to_tokens(cotangent)
+
+    mean1, inverse1 = stats(tokens)
+    rows1 = ((tokens - mean1) * inverse1 * gain1[:, None] + shift1[:, None]).astype(low)
+    mixed = (
+        jnp.einsum("pkn,kt->pnt", wide_qkv, rows1, preferred_element_type=f32)
+        + bias_qv[:, :, None]
+    ).astype(low)
+    mixed = mixed.reshape(HEADS, 3 * HEAD, rows)
+    attn, lse = attend(lengths, slopes, mixed)
+    attn = attn.reshape(HEADS * HEAD, rows)
+    flat_out = wide_out.reshape(HEADS * HEAD, -1)
+    hidden1 = (
+        tokens
+        + jnp.einsum("cd,ct->dt", flat_out, attn, preferred_element_type=f32)
+        + full_out[:, None]
+    )
+    mean2, inverse2 = stats(hidden1)
+    rows2 = ((hidden1 - mean2) * inverse2 * gain2[:, None] + shift2[:, None]).astype(low)
+    pre = (
+        jnp.einsum("pkn,kt->pnt", wide_up, rows2, preferred_element_type=f32)
+        + bias_hidden[:, :, None]
+    ).astype(low)
+    units = pre.shape[0] * pre.shape[1]
+    pre = pre.reshape(units, rows)
+    gelu = partial(jax.nn.gelu, approximate=True)
+    act = gelu(pre.astype(f32)).astype(low)
+    flat_down = wide_down.reshape(units, -1)
+    result = (
+        hidden1
+        + jnp.einsum("fd,ft->dt", flat_down, act, preferred_element_type=f32)
+        + full_down[:, None]
+    )
+    hidden_out = to_features(result)
+
+    def halves(equation, left, right, near_left, near_right):
+        def one(which):
+            pick = lambda value: value[which * (value.shape[0] // 2) :][: value.shape[0] // 2]
+            return jnp.einsum(
+                equation,
+                pick(left) if near_left else left,
+                pick(right) if near_right else right,
+                preferred_element_type=f32,
+            ).astype(low)
+
+        far = one(1)
+        return one(0), far
+
+    grad_low = grad_given.astype(low)
+    act8 = act.reshape(8, -1, rows)
+    sum_down = collect(
+        *halves("pft,dt->pfd", act8, grad_low, True, False), UP_ORDER
+    )
+    grad_act = jnp.einsum("fd,dt->ft", flat_down, grad_low, preferred_element_type=f32)
+    grad_pre = jax.vjp(gelu, pre.astype(f32))[1](grad_act)[0].astype(low)
+    pre8 = grad_pre.reshape(8, -1, rows)
+    sum_up = collect(*halves("kt,pnt->pkn", rows2, pre8, False, True), UP_ORDER)
+    grad_norm2 = jnp.einsum("pkn,pnt->kt", wide_up, pre8, preferred_element_type=f32)
+    normed2 = (hidden1 - mean2) * inverse2
+    grad_hidden1 = grad_given + norm_back(grad_norm2, normed2, inverse2, gain2[:, None])
+    branch_low = grad_hidden1.astype(low)
+    grad_attn = jnp.einsum("cd,dt->ct", flat_out, branch_low, preferred_element_type=f32)
+    grad_attn = grad_attn.astype(low).reshape(HEADS, HEAD, rows)
+    sum_out = collect(
+        *halves("pct,dt->pcd", attn.reshape(8, -1, rows), branch_low, True, False), HEAD_ORDER
+    )
+    grad_mixed = attend_back(lengths, slopes, mixed, grad_attn, lse)
+    mixed8 = grad_mixed.reshape(8, -1, rows)
+    sum_qkv = collect(*halves("kt,pnt->pkn", rows1, mixed8, False, True), HEAD_ORDER)
+    grad_norm1 = jnp.einsum("pkn,pnt->kt", wide_qkv, mixed8, preferred_element_type=f32)
+    normed1 = (tokens - mean1) * inverse1
+    grad_input = to_features(
+        grad_hidden1 + norm_back(grad_norm1, normed1, inverse1, gain1[:, None])
+    )
+
+    def total(value):
+        return jnp.sum(value, axis=1, dtype=f32)
+
+    head_back, up_back = jnp.argsort(head_at), jnp.argsort(up_at)
+    mixed_sums = jnp.sum(grad_mixed, axis=2, dtype=f32).reshape(8, pair_heads, 3, HEAD)[head_back]
+    early = (
+        total(grad_hidden1),
+        total(grad_norm2 * normed2),
+        total(grad_norm2),
+        total(grad_pre).reshape(8, -1)[up_back].reshape(-1),
+        total(grad_given),
+    )
+    late = (
+        total(grad_norm1 * normed1),
+        total(grad_norm1),
+        mixed_sums[:, :, 0].reshape(-1),
+        mixed_sums[:, :, 2].reshape(-1),
+    )
+
+    def reduce_small(values):
+        summed = lax.psum(jnp.concatenate([v.reshape(2, -1) for v in values], axis=1),
+                          ("dp", "row", "col"))
+        mine = lax.dynamic_slice_in_dim(summed, col, 1, 0)[0]
+        parts, at = [], 0
+        for value in values:
+            parts.append(mine[at : at + value.shape[0] // 2])
+            at += value.shape[0] // 2
+        return parts
+
+    g_bias_out, g_gain2, g_shift2, g_bias_up, g_bias_down = reduce_small(early)
+    g_gain1, g_shift1, g_bias_q, g_bias_v = reduce_small(late)
+
+    def finish(value, row_axis):
+        mine = lax.psum_scatter(value, "row", scatter_dimension=row_axis, tiled=True)
+        return lax.all_gather(mine, "dp", axis=1 - row_axis, tiled=True).astype(f32)
+
+    return (
+        hidden_out,
+        grad_input,
+        g_gain1,
+        g_shift1,
+        finish(sum_qkv, 0),
+        g_bias_q,
+        g_bias_v,
+        finish(sum_out, 1),
+        g_bias_out,
+        g_gain2,
+        g_shift2,
+        finish(sum_up, 0),
+        g_bias_up,
+        finish(sum_down, 1),
+        g_bias_down,
+    )
+
+
 def solution(mesh):
+    pairs = mesh.shape["col"] == 2 and mesh.shape["dp"] == 4
     return jax.shard_map(
-        body,
+        body if pairs else wide_body,
         mesh=mesh,
         in_specs=(
             P("col", ("dp", "row")),

time: 1340 us -> 750 us (0.56)
  waiting for transfers between devices: 733 us -> 204 us
  matrix products: 270 us -> 154 us
  Pallas kernels: 0 us -> 59.7 us
  other arithmetic: 124 us -> 87.8 us
  starting transfers between devices: 0.9 us -> 24 us
  blocking collectives: 90.2 us -> 107 us
    all_gather x8 -> x4, waiting for transfers between devices: 385 us -> 0.01 us  [the longest x2 0.01 us: finish(): return lax.all_gather(mine, 'dp', axis=1 - row_axis, tiled=True).astype(f32)]
    reduce_scatter x8 -> x4, waiting for transfers between devices: 294 us -> 0.01 us  [finish(): lax.psum_scatter(value, 'row', scatter_dimension=row_axis, tiled=True)]
    ppermute x0 -> x29, waiting for transfers between devices: none -> 204 us  [the longest x16 106 us: swap(): lax.ppermute(value, 'dp', [(i, i ^ step) for i in range(lax.axis_size('dp...]
    dot_general x40 -> x16, matrix products: 270 us -> 154 us  [the longest x8 40.8 us: one(): jnp.einsum(equation, pick(left) if near_left else left, pick(right) if ne...]
    pallas_call x0 -> x2, Pallas kernels: none -> 59.7 us  [the longest x1 35.4 us: attend_back(): pl.pallas_call(attend_back_kernel, grid_spec=pltpu.PrefetchScalarGridSpec...]
    all_gather x0 -> x4, blocking collectives: none -> 59.6 us  [the longest x1 27.1 us: body(): piece_qkv = lax.all_gather(quarter(w_qkv, 1), 'row', axis=0, tiled=True)]
    psum x1 -> x0, waiting for transfers between devices: 51.7 us -> none  [body(): lax.psum(local[0].astype(jnp.bfloat16), 'dp').astype(jnp.float32)]
    psum x5 -> x1, blocking collectives: 90.2 us -> 47.1 us  [reduce_small(): lax.psum(jnp.concatenate([v.reshape(2, -1) for v in values], axis=1), ('d...]
  transfers between devices with their start and end apart: 17 -> 37, of which waited for: 14 -> 11; matrix products, arithmetic and copies ran while one was open for 30% -> 36% of each run, Pallas kernels for 0% -> 8%
where the time goes in v1:
time: 750 us; the launch traced here: 740 us
  waiting for transfers between devices  204 us (27%)
  matrix products  154 us (21%)
  blocking collectives  107 us (14%)
  local copies, waits for them, and re-layouts  87.8 us (12%)
  other arithmetic  87.8 us (12%)
  Pallas kernels  59.7 us (8%)
  starting transfers between devices  24 us (3%)
  between operations  15.4 us (2%)
    ppermute x16, waiting for transfers between devices, swap(): lax.ppermute(value, 'dp', [(i, i ^ step) for i in range(lax.axis_size('dp...  106 us
    ppermute x13, waiting for transfers between devices, swap(): lax.ppermute(value, 'col', [(i, i ^ 1) for i in range(lax.axis_size('col'...  97.9 us
    psum x1, blocking collectives, reduce_small(): lax.psum(jnp.concatenate([v.reshape(2, -1) for v in values], axis=1), ('d...  47.1 us
    dot_general x8, matrix products, one(): jnp.einsum(equation, pick(left) if near_left else left, pick(right) if ne...  40.8 us
    unnamed x139, local copies, waits for them, and re-layouts  39.9 us
    pallas_call x1, Pallas kernels, attend_back(): pl.pallas_call(attend_back_kernel, grid_spec=pltpu.PrefetchScalarGridSpec...  35.4 us
    concatenate x10, other arithmetic, spread(): held = jnp.concatenate((held, swap(held, axis)), axis=0)  30.8 us
    dot_general x1, matrix products, body(): jnp.einsum('fd,dt->ft', flat_down, grad_low, preferred_element_type=f32)  27.3 us
  transfers between devices with their start and end apart: 37, of which 11 were waited for; matrix products, arithmetic and copies ran while one was open for 36% of the time, Pallas kernels for 8%

profile of v1, /device:TPU:0, one launch (start us, length us, event | category | flops | bytes accessed | tf_op | source)
XLA Modules:
  0.0 739.8 jit_solution(3764793706729488429)
XLA Ops:
  10.3 27.1 %all_gather.25 = bf16[1024,384]{0,1:T(8,128)(2,1)S(1)} all-gather(bf16[256,384]{0,1:T(8,128)(2,1)S(1)} %copy.109), channel_id=1, replica_groups=mesh['dp'=4,'row'=4,'col'=2] {'row'}, dimensions={0}, use_global_device_ids=true | all-gather | bytes 983040 | tf_op jit(solution)/shard_map/all_gather | solution.py:445
  56.6 16.8 %all_gather.24 = bf16[128,1024]{1,0:T(8,128)(2,1)S(1)} all-gather(bf16[128,256]{1,0:T(8,128)(2,1)S(1)} %constant_dynamic-slice_fusion.9), channel_id=1, replica_groups=mesh['dp'=4,'row'=4,'col'=2] {'row'}, dimensions={1}, use_global_device_ids=true | all-gather | bytes 327680 | tf_op jit(solution)/shard_map/all_gather | solution.py:446
  105.7 8.6 %collective-permute-done.8 = bf16[1,512,1024]{2,1,0:T(8,128)(2,1)} collective-permute-done((bf16[1,512,1024]{2,1,0:T(8,128)(2,1)}, bf16[1,512,1024]{2,1,0:T(8,128)(2,1)}, u32[]{:S(2)}, u32[]{:S(2)}) %collective-permute-start.8) | collective-permute-done | bytes 1048608 | tf_op jit(solution)/shard_map/ppermute | solution.py:372
  118.6 17.5 %collective-permute-done.11 = bf16[1,1024,512]{1,2,0:T(8,128)(2,1)} collective-permute-done((bf16[1,1024,512]{1,2,0:T(8,128)(2,1)}, bf16[1,1024,512]{1,2,0:T(8,128)(2,1)}, u32[]{:S(2)}, u32[]{:S(2)}) %collective-permute-start.11) | collective-permute-done | bytes 1048608 | tf_op jit(solution)/shard_map/ppermute | solution.py:372
  152.9 39.7 %collective-permute-done.9 = bf16[2,512,1024]{2,1,0:T(8,128)(2,1)} collective-permute-done((bf16[2,512,1024]{2,1,0:T(8,128)(2,1)}, bf16[2,512,1024]{2,1,0:T(8,128)(2,1)}, u32[]{:S(2)}, u32[]{:S(2)}) %collective-permute-start.9) | collective-permute-done | bytes 2097184 | tf_op jit(solution)/shard_map/ppermute | solution.py:370
  201.0 31.1 %collective-permute-done.12 = bf16[2,1024,512]{1,2,0:T(8,128)(2,1)} collective-permute-done((bf16[2,1024,512]{1,2,0:T(8,128)(2,1)}, bf16[2,1024,512]{1,2,0:T(8,128)(2,1)}, u32[]{:S(2)}, u32[]{:S(2)}) %collective-permute-start.12) | collective-permute-done | bytes 2097184 | tf_op jit(solution)/shard_map/ppermute | solution.py:370
  235.7 10.3 %add_convert_fusion.1 = bf16[8,384,1024]{2,1,0:T(8,128)(2,1)} fusion(f32[8,384]{1,0:T(8,128)S(1)} %gather_fusion, bf16[1024,1024,1]{0,1,2:T(8,128)(2,1)S(1)} %fusion.29, bf16[4,1024,384]{1,2,0:T(8,128)(2,1)} %collective-permute-done.6, bf16[2,1024,384]{1,2,0:T(8,128)(2,1)} %collective-permute-done.5, bf16[1,1024,384]{1,2,0:T(8,128)(2,1)S(1)} %copy-done.30, ...), kind=kOutput, calls=%fused_computation.30 | convolution fusion | flops 6458179584 | bytes 14692352 | tf_op jit(solution)/shard_map/pkn,kt->pnt/dot_general | solution.py:497
  246.0 24.3 %shard_map.271 = (bf16[16,64,1024]{2,1,0:T(8,128)(2,1)}, f32[16,1,1024]{2,1,0:T(1,128)}) custom-call(s32[2]{0:T(128)} %dynamic_slice.48.lengths, f32[16]{0:T(128)} %reshape.350.slopes, bf16[16,192,1024]{2,1,0:T(8,128)(2,1)} %bitcast.227), custom_call_target="tpu_custom_call" | custom-call | flops 8589934592 | bytes 16777216 | tf_op jit(solution)/shard_map/pallas_call | solution.py:331
  270.3 7.1 fusion.69
  278.2 8.2 %pad_maximum_fusion = bf16[8,512,1024]{2,1,0:T(8,128)(2,1)} fusion(bf16[4,512,1024]{2,1,0:T(8,128)(2,1)} %collective-permute-done.10, bf16[2,512,1024]{2,1,0:T(8,128)(2,1)} %collective-permute-done.9, bf16[1,512,1024]{2,1,0:T(8,128)(2,1)} %collective-permute-done.8, bf16[1,512,1024]{2,1,0:T(8,128)(2,1)S(1)} %bitcast.175), kind=kLoop, calls=%fused_computation.31 | loop fusion | flops 12582912 | bytes 16777216 | tf_op jit(solution)/shard_map/concatenate | solution.py:378
  286.4 13.3 %add_convert_fusion = bf16[8,512,1024]{2,1,0:T(8,128)(2,1)} fusion(bf16[1024,1024,1]{0,1,2:T(8,128)(2,1)S(1)} %fusion.30, f32[8,512]{1,0:T(8,128)S(1)} %gather_fusion.1, bf16[4,1024,512]{1,2,0:T(8,128)(2,1)} %collective-permute-done.13, bf16[2,1024,512]{1,2,0:T(8,128)(2,1)} %collective-permute-done.12, bf16[1,1024,512]{1,2,0:T(8,128)(2,1)} %collective-permute-done.11, ...), kind=kOutput, calls=%fused_computation.28 | convolution fusion | flops 8610906112 | bytes 18890752 | tf_op jit(solution)/shard_map/pkn,kt->pnt/dot_general | solution.py:512
  299.7 27.3 %convert_reduce_fusion = (f32[4096]{0:T(1024)}, bf16[4096,1024]{1,0:T(8,128)(2,1)}, bf16[4096,1024]{1,0:T(8,128)(2,1)}) fusion(bf16[8,512,1024]{2,1,0:T(8,128)(2,1)} %add_convert_fusion, bf16[4096,1024]{1,0:T(8,128)(2,1)} %bitcast.180, bf16[1024,1024]{0,1:T(8,128)(2,1)S(1)} %copy-done.35), kind=kOutput, calls=%fused_computation.27 | convolution fusion | flops 8694788096 | bytes 35667968 | tf_op jit(solution)/shard_map/fd,dt->ft/dot_general | solution.py:545
  332.3 6.1 convert_bitcast_fusion
  341.3 6.1 convolution_convert_fusion
  347.5 16.9 %fusion.23 = (f32[1024]{0:T(1024)S(1)}, f32[1024]{0:T(1024)S(1)}, f32[1024]{0:T(1024)S(1)}, f32[1024]{0:T(1024)S(1)}, f32[1024,1024,1]{0,1,2:T(8,128)}) fusion(f32[1024,1024]{0,1:T(8,128)} %copy-done.11, f32[1024]{0:T(1024)S(1)} %get-tuple-element.102, f32[1024]{0:T(1024)S(1)} %get-tuple-element.101, f32[1024]{0:T(1024)S(1)} %bitcast.210, ...), kind=kOutput, calls=%fused_computation.53 | convolution fusion | flops 8611950592 | bytes 25194496 | tf_op jit(solution)/shard_map/pkn,pnt->kt/dot_general | solution.py:549
  364.4 6.3 fusion.71
  375.8 6.3 fusion.18
  387.1 35.4 %shard_map.272 = bf16[16,192,1024]{2,1,0:T(8,128)(2,1)} custom-call(s32[2]{0:T(128)} %dynamic_slice.48.lengths, f32[16]{0:T(128)} %reshape.350.slopes, bf16[16,192,1024]{2,1,0:T(8,128)(2,1)} %bitcast.228, bf16[16,64,1024]{2,1,0:T(8,128)(2,1)} %bitcast.229, f32[16,1,1024]{2,1,0:T(1,128)} %get-tuple-element.20.lse_ref), custom_call_target="tpu_custom_call" | custom-call | flops 21474836480 | bytes 33554432 | tf_op jit(solution)/shard_map/pallas_call | solution.py:353
  422.5 5.8 fusion.74
  428.4 6.3 add_convert_fusion.2
  447.1 19.9 %collective-permute-done.25 = bf16[1,1024,512]{1,2,0:T(8,128)(2,1)S(1)} collective-permute-done((bf16[1,1024,512]{1,2,0:T(8,128)(2,1)S(1)}, bf16[1,1024,512]{1,2,0:T(8,128)(2,1)S(1)}, u32[]{:S(2)}, u32[]{:S(2)}) %collective-permute-start.25) | collective-permute-done | bytes 1048608 | tf_op jit(solution)/shard_map/ppermute | solution.py:372
  468.5 15.7 %collective-permute-done.27 = bf16[2,512,1024]{2,1,0:T(8,128)(2,1)} collective-permute-done((bf16[2,512,1024]{2,1,0:T(8,128)(2,1)}, bf16[2,512,1024]{2,1,0:T(8,128)(2,1)}, u32[]{:S(2)}, u32[]{:S(2)}) %collective-permute-start.27) | collective-permute-done | bytes 2097184 | tf_op jit(solution)/shard_map/ppermute | solution.py:370
  492.3 19.8 %collective-permute-done.28 = bf16[1,512,1024]{2,1,0:T(8,128)(2,1)S(1)} collective-permute-done((bf16[1,512,1024]{2,1,0:T(8,128)(2,1)S(1)}, bf16[1,512,1024]{2,1,0:T(8,128)(2,1)S(1)}, u32[]{:S(2)}, u32[]{:S(2)}) %collective-permute-start.28) | collective-permute-done | bytes 1048608 | tf_op jit(solution)/shard_map/ppermute | solution.py:372
  513.5 6.2 fusion.21
  526.5 39.4 %collective-permute-done.21 = bf16[2,128,1024]{2,1,0:T(8,128)(2,1)} collective-permute-done((bf16[2,128,1024]{2,1,0:T(8,128)(2,1)S(1)}, bf16[2,128,1024]{2,1,0:T(8,128)(2,1)}, u32[]{:S(2)}, u32[]{:S(2)}) %collective-permute-start.21) | collective-permute-done | bytes 524320 | tf_op jit(solution)/shard_map/ppermute | solution.py:372
  568.5 6.0 collective-permute-done.22
  581.1 20.4 %fusion.24 = f32[1024,1024]{0,1:T(8,128)} fusion(f32[1024,1024]{0,1:T(8,128)} %copy-done.11, bf16[8,512,1024]{2,1,0:T(8,128)(2,1)} %add_convert_fusion, f32[1024]{0:T(1024)S(1)} %bitcast.218, bf16[4,512,1024]{2,1,0:T(8,128)(2,1)} %collective-permute-done.10, bf16[2,512,1024]{2,1,0:T(8,128)(2,1)} %collective-permute-done.9, ...), kind=kOutput, calls=%fused_computation.55 | convolution fusion | flops 8646557696 | bytes 25169920 | tf_op jit(solution)/shard_map/fd,ft->dt/dot_general | solution.py:522
  608.6 14.2 %fusion.22 = (f32[1024]{0:T(1024)S(1)}, f32[1024]{0:T(1024)S(1)}, f32[1024]{0:T(1024)S(1)}, f32[1024]{0:T(1024)S(1)}, f32[1024,1024,1]{0,1,2:T(8,128)}) fusion(f32[1024]{0:T(1024)S(1)} %copy-done.47, f32[1024]{0:T(1024)S(1)} %copy-done.45, f32[512,1024]{0,1:T(8,128)S(1)} %copy-done.3, f32[512,1024]{0,1:T(8,128)} %copy-done.4, pred[]{:T(512)S(6)} %eq.12, ...), kind=kOutput, calls=%fused_computation.49 | convolution fusion | flops 6464466944 | bytes 21000192 | tf_op jit(solution)/shard_map/pkn,pnt->kt/dot_general | solution.py:561
  622.8 7.5 %multiply_add_fusion = f32[1024,1024]{0,1:T(8,128)} fusion(f32[1024,1024]{0,1:T(8,128)} %copy-done.8, f32[1024,1024,1]{0,1,2:T(8,128)} %get-tuple-element.107, f32[1024]{0:T(1024)S(1)} %broadcast_multiply_fusion, f32[1024]{0:T(1024)S(1)} %broadcast_multiply_fusion.1, f32[1024]{0:T(1024)S(1)} %bitcast.208, f32[1024]{0:T(1024)S(1)} %copy-done.47, ...), kind=kLoop, calls=%fused_computation.59 | loop fusion | flops 11534336 | bytes 16797696 | tf_op jit(solution)/shard_map/add | solution.py:564
  638.9 47.1 %all-reduce = (f32[2,2048]{1,0:T(2,128)S(1)}, f32[2,4096]{1,0:T(2,128)S(1)}) all-reduce(f32[2,2048]{1,0:T(2,128)S(1)} %pad_maximum_fusion.17, f32[2,4096]{1,0:T(2,128)S(1)} %constant_dynamic-update-slice_fusion.1), channel_id=1, replica_groups=mesh['dp'=4,'row'=4,'col'=2] {'dp','row','col'}, use_global_device_ids=true, to_apply=%region_12.13 | all-reduce | flops 12288 | bytes 98304 | tf_op jit(solution)/shard_map/psum | solution.py:587
  709.6 6.6 all_gather.29
  717.0 9.0 %all_gather.28 = bf16[256,1536]{0,1:T(8,128)(2,1)S(1)} all-gather(bf16[256,384]{0,1:T(8,128)(2,1)} %reduce-scatter.5.cloned.1.call-done), channel_id=1, replica_groups=mesh['dp'=4,'row'=4,'col'=2] {'dp'}, dimensions={1}, use_global_device_ids=true | all-gather | bytes 983040 | tf_op jit(solution)/shard_map/all_gather | solution.py:601
  (323 shorter events, 192.0 us)
Async XLA Ops:
  7.2 75.7 %all-gather.5.cloned.1.call-start = ((), (), s32[]{:S(2)}) async-start(), calls=%async_computation.4 | async-start | bytes 1310720 | tf_op jit(solution)/shard_map/all_gather | solution.py:448
  9.2 77.9 %all-gather.7.cloned.1.call-start = ((), (), s32[]{:S(2)}) async-start(), calls=%async_computation.5 | async-start | bytes 1310720 | tf_op jit(solution)/shard_map/all_gather | solution.py:447
  40.8 589.5 %reduce-scatter.9.cloned.1.call-start = ((), (), s32[]{:S(2)}) async-start(), calls=%async_computation.8 | async-start | bytes 1310720 | tf_op jit(solution)/shard_map/reduce_scatter | solution.py:600
  47.0 71.6 %collective-permute-start.7 = (f32[6144]{0:T(1024)S(1)}, f32[6144]{0:T(1024)S(1)}, u32[]{:S(2)}, u32[]{:S(2)}) collective-permute-start(f32[6144]{0:T(1024)S(1)} %constant_dynamic-update-slice_fusion.6), channel_id=1, source_target_pairs={{0,1},{1,0},{2,3},{3,2},{4,5},{5,4},{6,7},{7,6},{8,9},{9,8},{10,11... | collective-permute-start | bytes 73736 | tf_op jit(solution)/shard_map/ppermute | solution.py:370
  54.3 45.9 %collective-permute-start.5 = (bf16[2,1024,384]{1,2,0:T(8,128)(2,1)}, bf16[2,1024,384]{1,2,0:T(8,128)(2,1)}, u32[]{:S(2)}, u32[]{:S(2)}) collective-permute-start(bf16[2,1024,384]{1,2,0:T(8,128)(2,1)} %pad_maximum_fusion.9), channel_id=1, source_target_pairs={{0,16},{8,24},{16,0},{24,8},{1,17},{9,25},{17,1},{25,9},{2,18},{10... | collective-permute-start | bytes 4718600 | tf_op jit(solution)/shard_map/ppermute | solution.py:372
  82.9 31.3 %collective-permute-start.8 = (bf16[1,512,1024]{2,1,0:T(8,128)(2,1)}, bf16[1,512,1024]{2,1,0:T(8,128)(2,1)}, u32[]{:S(2)}, u32[]{:S(2)}) collective-permute-start(bf16[1,512,1024]{2,1,0:T(8,128)(2,1)} %bitcast.172), channel_id=1, source_target_pairs={{0,16},{8,24},{16,0},{24,8},{1,17},{9,25},{17,1},{25,9},{2,18},{10... | collective-permute-start | bytes 3145736 | tf_op jit(solution)/shard_map/ppermute | solution.py:372
  87.1 49.1 %collective-permute-start.11 = (bf16[1,1024,512]{1,2,0:T(8,128)(2,1)}, bf16[1,1024,512]{1,2,0:T(8,128)(2,1)}, u32[]{:S(2)}, u32[]{:S(2)}) collective-permute-start(bf16[1,1024,512]{1,2,0:T(8,128)(2,1)} %bitcast.194), channel_id=1, source_target_pairs={{0,16},{8,24},{16,0},{24,8},{1,17},{9,25},{17,1},{25,9},{2,18},{10... | collective-permute-start | bytes 3145736 | tf_op jit(solution)/shard_map/ppermute | solution.py:372
  98.7 48.0 %collective-permute-start = (bf16[512,1024]{0,1:T(8,128)(2,1)}, bf16[512,1024]{0,1:T(8,128)(2,1)}, u32[]{:S(2)}, u32[]{:S(2)}) collective-permute-start(bf16[512,1024]{0,1:T(8,128)(2,1)} %copy.108), channel_id=1, source_target_pairs={{0,1},{1,0},{2,3},{3,2},{4,5},{5,4},{6,7},{7,6},{8,9},{9,8},{10,11... | collective-permute-start | bytes 3145736 | tf_op jit(solution)/shard_map/ppermute | solution.py:370
  100.1 48.1 %collective-permute-start.15 = (bf16[512,1024]{0,1:T(8,128)(2,1)}, bf16[512,1024]{0,1:T(8,128)(2,1)}, u32[]{:S(2)}, u32[]{:S(2)}) collective-permute-start(bf16[512,1024]{0,1:T(8,128)(2,1)} %copy.112), channel_id=1, source_target_pairs={{0,1},{1,0},{2,3},{3,2},{4,5},{5,4},{6,7},{7,6},{8,9},{9,8},{10,11... | collective-permute-start | bytes 3145736 | tf_op jit(solution)/shard_map/ppermute | solution.py:370
  114.2 27.5 %collective-permute-start.2 = (bf16[2,128,1024]{2,1,0:T(8,128)(2,1)S(1)}, bf16[2,128,1024]{2,1,0:T(8,128)(2,1)}, u32[]{:S(2)}, u32[]{:S(2)}) collective-permute-start(bf16[2,128,1024]{2,1,0:T(8,128)(2,1)S(1)} %pad_maximum_fusion.15), channel_id=1, source_target_pairs={{0,16},{8,24},{16,0},{24,8},{1,17},{9,25},{17,1},{25,9},{2,18},{10... | collective-permute-start | bytes 1572872 | tf_op jit(solution)/shard_map/ppermute | solution.py:372
  118.6 117.0 %collective-permute-start.6 = (bf16[4,1024,384]{1,2,0:T(8,128)(2,1)}, bf16[4,1024,384]{1,2,0:T(8,128)(2,1)}, u32[]{:S(2)}, u32[]{:S(2)}) collective-permute-start(bf16[4,1024,384]{1,2,0:T(8,128)(2,1)} %pad_maximum_fusion.5), channel_id=1, source_target_pairs={{0,8},{8,0},{16,24},{24,16},{1,9},{9,1},{17,25},{25,17},{2,10},{10... | collective-permute-start | bytes 9437192 | tf_op jit(solution)/shard_map/ppermute | solution.py:372
  136.2 56.4 %collective-permute-start.9 = (bf16[2,512,1024]{2,1,0:T(8,128)(2,1)}, bf16[2,512,1024]{2,1,0:T(8,128)(2,1)}, u32[]{:S(2)}, u32[]{:S(2)}) collective-permute-start(bf16[2,512,1024]{2,1,0:T(8,128)(2,1)} %pad_maximum_fusion.7), channel_id=1, source_target_pairs={{0,1},{1,0},{2,3},{3,2},{4,5},{5,4},{6,7},{7,6},{8,9},{9,8},{10,11... | collective-permute-start | bytes 6291464 | tf_op jit(solution)/shard_map/ppermute | solution.py:370
  141.8 90.3 %collective-permute-start.12 = (bf16[2,1024,512]{1,2,0:T(8,128)(2,1)}, bf16[2,1024,512]{1,2,0:T(8,128)(2,1)}, u32[]{:S(2)}, u32[]{:S(2)}) collective-permute-start(bf16[2,1024,512]{1,2,0:T(8,128)(2,1)} %pad_maximum_fusion.8), channel_id=1, source_target_pairs={{0,1},{1,0},{2,3},{3,2},{4,5},{5,4},{6,7},{7,6},{8,9},{9,8},{10,11... | collective-permute-start | bytes 6291464 | tf_op jit(solution)/shard_map/ppermute | solution.py:370
  146.6 51.7 %collective-permute-start.3 = (bf16[4,128,1024]{2,1,0:T(8,128)(2,1)S(1)}, bf16[4,128,1024]{2,1,0:T(8,128)(2,1)S(1)}, u32[]{:S(2)}, u32[]{:S(2)}) collective-permute-start(bf16[4,128,1024]{2,1,0:T(8,128)(2,1)S(1)} %pad_maximum_fusion.14), channel_id=1, source_target_pairs={{0,8},{8,0},{16,24},{24,16},{1,9},{9,1},{17,25},{25,17},{2,10},{10... | collective-permute-start | bytes 3145736 | tf_op jit(solution)/shard_map/ppermute | solution.py:372
  196.1 82.1 %collective-permute-start.10 = (bf16[4,512,1024]{2,1,0:T(8,128)(2,1)}, bf16[4,512,1024]{2,1,0:T(8,128)(2,1)}, u32[]{:S(2)}, u32[]{:S(2)}) collective-permute-start(bf16[4,512,1024]{2,1,0:T(8,128)(2,1)} %pad_maximum_fusion.3), channel_id=1, source_target_pairs={{0,8},{8,0},{16,24},{24,16},{1,9},{9,1},{17,25},{25,17},{2,10},{10... | collective-permute-start | bytes 12582920 | tf_op jit(solution)/shard_map/ppermute | solution.py:372
  235.6 50.8 %collective-permute-start.13 = (bf16[4,1024,512]{1,2,0:T(8,128)(2,1)}, bf16[4,1024,512]{1,2,0:T(8,128)(2,1)}, u32[]{:S(2)}, u32[]{:S(2)}) collective-permute-start(bf16[4,1024,512]{1,2,0:T(8,128)(2,1)} %pad_maximum_fusion.4), channel_id=1, source_target_pairs={{0,8},{8,0},{16,24},{24,16},{1,9},{9,1},{17,25},{25,17},{2,10},{10... | collective-permute-start | bytes 12582920 | tf_op jit(solution)/shard_map/ppermute | solution.py:372
  338.4 36.0 %collective-permute-start.23 = (bf16[4,1024,512]{1,2,0:T(8,128)(2,1)}, bf16[4,1024,512]{1,2,0:T(8,128)(2,1)}, u32[]{:S(2)}, u32[]{:S(2)}) collective-permute-start(bf16[4,1024,512]{1,2,0:T(8,128)(2,1)} %convert_bitcast_fusion), channel_id=1, source_target_pairs={{0,8},{8,0},{16,24},{24,16},{1,9},{9,1},{17,25},{25,17},{2,10},{10... | collective-permute-start | bytes 12582920 | tf_op jit(solution)/shard_map/ppermute | solution.py:372
  347.4 80.9 %collective-permute-start.26 = (bf16[4,512,1024]{2,1,0:T(8,128)(2,1)}, bf16[4,512,1024]{2,1,0:T(8,128)(2,1)}, u32[]{:S(2)}, u32[]{:S(2)}) collective-permute-start(bf16[4,512,1024]{2,1,0:T(8,128)(2,1)} %convolution_convert_fusion), channel_id=1, source_target_pairs={{0,8},{8,0},{16,24},{24,16},{1,9},{9,1},{17,25},{25,17},{2,10},{10... | collective-permute-start | bytes 12582920 | tf_op jit(solution)/shard_map/ppermute | solution.py:372
  385.6 51.1 %collective-permute-start.24 = (bf16[2,1024,512]{1,2,0:T(8,128)(2,1)}, bf16[2,1024,512]{1,2,0:T(8,128)(2,1)}, u32[]{:S(2)}, u32[]{:S(2)}) collective-permute-start(bf16[2,1024,512]{1,2,0:T(8,128)(2,1)} %slice.276), channel_id=1, source_target_pairs={{0,1},{1,0},{2,3},{3,2},{4,5},{5,4},{6,7},{7,6},{8,9},{9,8},{10,11... | collective-permute-start | bytes 6291464 | tf_op jit(solution)/shard_map/ppermute | solution.py:370
  436.2 48.0 %collective-permute-start.27 = (bf16[2,512,1024]{2,1,0:T(8,128)(2,1)}, bf16[2,512,1024]{2,1,0:T(8,128)(2,1)}, u32[]{:S(2)}, u32[]{:S(2)}) collective-permute-start(bf16[2,512,1024]{2,1,0:T(8,128)(2,1)} %slice.282), channel_id=1, source_target_pairs={{0,1},{1,0},{2,3},{3,2},{4,5},{5,4},{6,7},{7,6},{8,9},{9,8},{10,11... | collective-permute-start | bytes 6291464 | tf_op jit(solution)/shard_map/ppermute | solution.py:370
  441.7 25.3 %collective-permute-start.25 = (bf16[1,1024,512]{1,2,0:T(8,128)(2,1)S(1)}, bf16[1,1024,512]{1,2,0:T(8,128)(2,1)S(1)}, u32[]{:S(2)}, u32[]{:S(2)}) collective-permute-start(bf16[1,1024,512]{1,2,0:T(8,128)(2,1)S(1)} %slice.278), channel_id=1, source_target_pairs={{0,16},{8,24},{16,0},{24,8},{1,17},{9,25},{17,1},{25,9},{2,18},{10... | collective-permute-start | bytes 3145736 | tf_op jit(solution)/shard_map/ppermute | solution.py:372
  447.1 66.3 %collective-permute-start.17 = (bf16[4,1024,384]{1,2,0:T(8,128)(2,1)}, bf16[4,1024,384]{1,2,0:T(8,128)(2,1)}, u32[]{:S(2)}, u32[]{:S(2)}) collective-permute-start(bf16[4,1024,384]{1,2,0:T(8,128)(2,1)} %convert_bitcast_fusion.1), channel_id=1, source_target_pairs={{0,8},{8,0},{16,24},{24,16},{1,9},{9,1},{17,25},{25,17},{2,10},{10... | collective-permute-start | bytes 9437192 | tf_op jit(solution)/shard_map/ppermute | solution.py:372
  468.4 218.3 %reduce-scatter.11.cloned.1.call-start = ((), (), s32[]{:S(2)}) async-start(), calls=%async_computation.10 | async-start | bytes 1310720 | tf_op jit(solution)/shard_map/reduce_scatter | solution.py:600
  492.3 28.2 %collective-permute-start.20 = (bf16[4,128,1024]{2,1,0:T(8,128)(2,1)}, bf16[4,128,1024]{2,1,0:T(8,128)(2,1)}, u32[]{:S(2)}, u32[]{:S(2)}) collective-permute-start(bf16[4,128,1024]{2,1,0:T(8,128)(2,1)} %fusion.40), channel_id=1, source_target_pairs={{0,8},{8,0},{16,24},{24,16},{1,9},{9,1},{17,25},{25,17},{2,10},{10... | collective-permute-start | bytes 3145736 | tf_op jit(solution)/shard_map/ppermute | solution.py:372
  513.4 196.2 %reduce-scatter.7.cloned.1.call-start = ((), (), s32[]{:S(2)}) async-start(), calls=%async_computation.7 | async-start | bytes 327680 | tf_op jit(solution)/shard_map/reduce_scatter | solution.py:600
  519.8 56.0 %collective-permute-start.18 = (bf16[2,1024,384]{1,2,0:T(8,128)(2,1)S(1)}, bf16[2,1024,384]{1,2,0:T(8,128)(2,1)}, u32[]{:S(2)}, u32[]{:S(2)}) collective-permute-start(bf16[2,1024,384]{1,2,0:T(8,128)(2,1)S(1)} %slice.266), channel_id=1, source_target_pairs={{0,16},{8,24},{16,0},{24,8},{1,17},{9,25},{17,1},{25,9},{2,18},{10... | collective-permute-start | bytes 4718600 | tf_op jit(solution)/shard_map/ppermute | solution.py:372
  523.4 42.6 %collective-permute-start.21 = (bf16[2,128,1024]{2,1,0:T(8,128)(2,1)S(1)}, bf16[2,128,1024]{2,1,0:T(8,128)(2,1)}, u32[]{:S(2)}, u32[]{:S(2)}) collective-permute-start(bf16[2,128,1024]{2,1,0:T(8,128)(2,1)S(1)} %slice.270), channel_id=1, source_target_pairs={{0,16},{8,24},{16,0},{24,8},{1,17},{9,25},{17,1},{25,9},{2,18},{10... | collective-permute-start | bytes 1572872 | tf_op jit(solution)/shard_map/ppermute | solution.py:372
  575.3 141.7 %reduce-scatter.5.cloned.1.call-start = ((), (), s32[]{:S(2)}) async-start(), calls=%async_computation.6 | async-start | bytes 983040 | tf_op jit(solution)/shard_map/reduce_scatter | solution.py:600
  604.3 85.8 %collective-permute-start.14 = (bf16[512,1024]{0,1:T(8,128)(2,1)}, bf16[512,1024]{0,1:T(8,128)(2,1)}, u32[]{:S(2)}, u32[]{:S(2)}) collective-permute-start(bf16[512,1024]{0,1:T(8,128)(2,1)} %dynamic-slice_convert_fusion.1), channel_id=1, source_target_pairs={{0,1},{1,0},{2,3},{3,2},{4,5},{5,4},{6,7},{7,6},{8,9},{9,8},{10,11... | collective-permute-start | bytes 3145736 | tf_op jit(solution)/shard_map/ppermute | solution.py:370
  608.5 119.0 %all-gather.9.cloned.1.call-start = ((), (), s32[]{:S(2)}) async-start(), calls=%async_computation.9 | async-start | bytes 1310720 | tf_op jit(solution)/shard_map/all_gather | solution.py:601
  630.3 99.8 %all-gather.11.cloned.1.call-start = ((), (), s32[]{:S(2)}) async-start(), calls=%async_computation.11 | async-start | bytes 1310720 | tf_op jit(solution)/shard_map/all_gather | solution.py:601
  633.0 66.9 %collective-permute-start.16 = (bf16[512,1024]{0,1:T(8,128)(2,1)}, bf16[512,1024]{0,1:T(8,128)(2,1)}, u32[]{:S(2)}, u32[]{:S(2)}) collective-permute-start(bf16[512,1024]{0,1:T(8,128)(2,1)} %dynamic-slice_convert_fusion), channel_id=1, source_target_pairs={{0,1},{1,0},{2,3},{3,2},{4,5},{5,4},{6,7},{7,6},{8,9},{9,8},{10,11... | collective-permute-start | bytes 3145736 | tf_op jit(solution)/shard_map/ppermute | solution.py:370
  (60 other events, 1153.2 us)
Sparse Core Ops, SparseCore 0:
  10.2 37.7 all-gather.4
  50.1 32.3 all-gather.6
  468.6 25.4 reduce-scatter.8
  513.5 25.4 reduce-scatter.10
  575.4 17.9 reduce-scatter.6
  608.6 21.5 reduce-scatter.4
  631.9 16.3 all-gather.8
  686.9 17.3 all-gather.10
